TPU v7x, 128 devices: a whole 4x4x4 slice. The times are simulated.
128 devices in a mesh: ctx: 8 (over z, x_hi), tp: 16 (over x_lo, y, core).
Axes of the slice: x: 4 (x_hi: 2, x_lo: 2; x = x_hi * 2 + x_lo), y: 4, z: 4, core: 2. Of those that a mesh axis runs over, the one named last changes fastest.
Arguments:
- residual_in: bfloat16 [1024, 8192], P('ctx', 'tp'), may hold values from -0.3 to 0.3
- dh_rest: bfloat16 [1024, 8192], P('ctx', 'tp'), may hold values from -0.29882812 to 0.29882812
- w_query: bfloat16 [8192, 8192], P(None, 'tp'), may hold values from -0.0625 to 0.0625
- w_key: bfloat16 [8192, 1024], P(None, 'tp'), may hold values from -0.0625 to 0.0625
- w_value: bfloat16 [8192, 1024], P(None, 'tp'), may hold values from -0.0625 to 0.0625
- q_raw: bfloat16 [1024, 8192], P('ctx', 'tp'), may hold values from -33 to 33
- k_raw: bfloat16 [1024, 1024], P('ctx'), may hold values from -33 to 33
- v_win: bfloat16 [1024, 1024], P('ctx'), may hold values from -6 to 6
- cache_k: bfloat16 [8192, 1024], P('ctx'), may hold values from -90 to 90
- cache_v: bfloat16 [8192, 1024], P('ctx'), may hold values from -6 to 6
- d_attn: bfloat16 [1024, 8192], P('ctx', 'tp'), may hold values from -6 to 6
- s_qk: float32 [128], replicated, may hold values from 0.8 to 5.5
- cache_live: int32 [1], replicated, may hold values from 4096 to 8192
Outputs:
- grad_input: float32 [1024, 8192], P('ctx', 'tp')
All inputs are finite; a program needn't handle non-finite values.
Results may differ from a plain program's by a relative error of at most 0.0025.
The roundings to bfloat16 on the way count: a program that leaves them out, or rounds other values in their place, can miss the bound.
Values may be sent and summed in bfloat16 or wider, within the bound.
No kernel may reach another device: no remote copies, remote signals or barrier semaphores. Data moves between devices by JAX's collectives and lax.ppermute only.
A program may use at most 128 MiB of HBM per device.

v0:
```python
import math
import jax
import jax.numpy as jnp
from jax import lax
from jax.sharding import PartitionSpec as P

D = 8192
KVH = 8
HD = 128
EPS = 1e-06


def swapped(block, axis, apart):
    count = lax.axis_size(axis)
    route = []
    for low in range(count):
        high = low | 1 << apart
        if high != low and high < count:
            route += [(low, high), (high, low)]
    return lax.ppermute(block, axis, route)


def unit_rows(values, qk_gain):
    width = values.shape[-1]
    mean_sq = jnp.mean(values * values, axis=-1, keepdims=True)
    return values * (lax.rsqrt(mean_sq + EPS) / math.sqrt(width)) * qk_gain


def unit_back(values, qk_gain, grad):
    width = values.shape[-1]
    mean_sq = jnp.mean(values * values, axis=-1, keepdims=True)
    factor = lax.rsqrt(mean_sq + EPS) / math.sqrt(width)
    weighted = qk_gain * grad
    inner = jnp.sum(weighted * values, axis=-1, keepdims=True)
    return factor * (weighted - values * inner / (width * (mean_sq + EPS)))


def contract_last(left, right):
    return lax.dot_general(
        left, right, (((1,), (1,)), ((), ())), preferred_element_type=jnp.float32
    )


def contract_first(left, right):
    return lax.dot_general(
        left, right, (((0,), (0,)), ((), ())), preferred_element_type=jnp.float32
    )


def on_device(
    residual_in,
    dh_rest,
    w_query,
    w_key,
    w_value,
    q_raw,
    k_raw,
    v_win,
    cache_k,
    cache_v,
    d_attn,
    s_qk,
    cache_live,
):
    tok_rows = q_raw.shape[0]
    ctx_count = lax.axis_size("ctx")
    tp_count = lax.axis_size("tp")
    head_count = q_raw.shape[1] // HD
    group_size = tp_count // KVH
    tp_index = lax.axis_index("tp")
    ctx_index = lax.axis_index("ctx")
    group_index = tp_index // group_size
    member = tp_index % group_size
    cache_rows = cache_k.shape[0]
    total_cache = cache_rows * ctx_count
    total_tokens = tok_rows * ctx_count
    score_scale = math.sqrt(HD)
    key_raw = lax.dynamic_slice_in_dim(k_raw, group_index * HD, HD, 1).astype(jnp.float32)
    window_pack = jnp.concatenate(
        [
            unit_rows(key_raw, s_qk).astype(jnp.bfloat16),
            lax.dynamic_slice_in_dim(v_win, group_index * HD, HD, 1),
        ],
        1,
    )
    raw_keys = lax.dynamic_slice(cache_k, (0, group_index * HD), (cache_rows, HD)).astype(
        jnp.float32
    )
    raw_values = lax.dynamic_slice(cache_v, (0, group_index * HD), (cache_rows, HD))
    all_cache = lax.all_gather(
        jnp.concatenate([unit_rows(raw_keys, s_qk).astype(jnp.bfloat16), raw_values], 1),
        "ctx",
        axis=0,
        tiled=True,
    )
    all_window = lax.all_gather(window_pack, "ctx", axis=0, tiled=True)
    query_raw = q_raw.astype(jnp.float32).reshape(tok_rows, head_count, HD)
    row_total = head_count * tok_rows
    query_rows = (
        unit_rows(query_raw, s_qk).astype(jnp.bfloat16).transpose(1, 0, 2).reshape(row_total, HD)
    )
    dout_rows = d_attn.reshape(tok_rows, head_count, HD).transpose(1, 0, 2).reshape(row_total, HD)
    query_pos = (
        total_cache + ctx_index * tok_rows + jnp.arange(row_total, dtype=jnp.int32) % tok_rows
    )
    floor_pos = total_cache - cache_live[0]
    all_keys = jnp.concatenate([all_cache, all_window], 0)
    block = math.gcd(math.gcd(1024, total_cache), total_tokens)
    key_blocks = all_keys[:, :HD].reshape(-1, block, HD)
    value_blocks = all_keys[:, HD:].reshape(-1, block, HD)
    block_starts = jnp.arange(key_blocks.shape[0], dtype=jnp.int32) * block
    cache_blocks = total_cache // block

    def block_scores(key_block, start):
        scores = contract_last(query_rows, key_block) * score_scale
        key_pos = start + jnp.arange(block, dtype=jnp.int32)
        visible = (key_pos[None, :] >= floor_pos) & (key_pos[None, :] <= query_pos[:, None])
        return (scores, visible)

    def stat_step(carry, inputs):
        row_max, row_sum, weighted = carry
        key_block, value_block, start = inputs
        scores, visible = block_scores(key_block, start)
        dprobs = contract_last(dout_rows, value_block)
        new_max = jnp.maximum(row_max, jnp.max(jnp.where(visible, scores, -1e30), axis=1))
        rescale = jnp.exp(row_max - new_max)
        expo = jnp.where(visible, jnp.exp(scores - new_max[:, None]), 0.0)
        row_sum = row_sum * rescale + jnp.sum(expo, axis=1)
        weighted = weighted * rescale + jnp.sum(expo * dprobs, axis=1)
        return ((new_max, row_sum, weighted), None)

    start_max = jnp.full((row_total,), -1e30, jnp.float32)
    start_zero = jnp.zeros((row_total,), jnp.float32)
    (row_max, row_sum, weighted), _ = lax.scan(
        stat_step, (start_max, start_zero, start_zero), (key_blocks, value_blocks, block_starts)
    )
    lse = row_max + jnp.log(row_sum)
    delta = weighted / row_sum

    def block_grads(key_block, value_block, start):
        scores, visible = block_scores(key_block, start)
        probs = jnp.where(visible, jnp.exp(scores - lse[:, None]), 0.0)
        dprobs = contract_last(dout_rows, value_block)
        dscores = (probs * (dprobs - delta[:, None])).astype(jnp.bfloat16)
        return (probs, dscores)

    def cache_step(dq_total, inputs):
        key_block, value_block, start = inputs
        probs, dscores = block_grads(key_block, value_block, start)
        return (
            dq_total
            + jnp.dot(dscores, key_block, preferred_element_type=jnp.float32) * score_scale,
            None,
        )

    def window_step(dq_total, inputs):
        key_block, value_block, start = inputs
        probs, dscores = block_grads(key_block, value_block, start)
        dq_total = (
            dq_total + jnp.dot(dscores, key_block, preferred_element_type=jnp.float32) * score_scale
        )
        key_grad = contract_first(dscores, query_rows) * score_scale
        value_grad = contract_first(probs.astype(jnp.bfloat16), dout_rows)
        return (dq_total, jnp.concatenate([key_grad, value_grad], 1))

    dq_rows = jnp.zeros((row_total, HD), jnp.float32)
    dq_rows, _ = lax.scan(
        cache_step,
        dq_rows,
        (key_blocks[:cache_blocks], value_blocks[:cache_blocks], block_starts[:cache_blocks]),
    )
    dq_rows, window_parts = lax.scan(
        window_step,
        dq_rows,
        (key_blocks[cache_blocks:], value_blocks[cache_blocks:], block_starts[cache_blocks:]),
    )
    window_grads = window_parts.reshape(total_tokens, 2 * HD)
    own_grads = lax.psum_scatter(window_grads, "ctx", scatter_dimension=0, tiled=True)
    own_grads = own_grads + swapped(own_grads, "tp", 0)
    key_cols = w_key.shape[1]
    grad_k_full = unit_back(key_raw, s_qk, own_grads[:, :HD]).astype(jnp.bfloat16)
    grad_v_full = own_grads[:, HD:].astype(jnp.bfloat16)
    grad_k = lax.dynamic_slice_in_dim(grad_k_full, member * key_cols, key_cols, 1)
    grad_v = lax.dynamic_slice_in_dim(grad_v_full, member * key_cols, key_cols, 1)
    dq_heads = dq_rows.reshape(head_count, tok_rows, HD).transpose(1, 0, 2)
    grad_q = (
        unit_back(query_raw, s_qk, dq_heads).astype(jnp.bfloat16).reshape(tok_rows, head_count * HD)
    )
    slab = lax.psum_scatter(
        contract_last(w_query, grad_q)
        + contract_last(w_key, grad_k)
        + contract_last(w_value, grad_v),
        "tp",
        scatter_dimension=0,
        tiled=True,
    )
    grad_total = slab.T + dh_rest.astype(jnp.float32)
    resid = residual_in.astype(jnp.float32)
    square_sum, inner_sum = lax.psum(
        (jnp.sum(resid * resid, axis=1), jnp.sum(grad_total * resid, axis=1)), "tp"
    )
    mean_sq = square_sum / D
    factor = lax.rsqrt(mean_sq + EPS) / math.sqrt(D)
    correction = inner_sum / (D * (mean_sq + EPS))
    return factor[:, None] * (grad_total - resid * correction[:, None])


def solution(mesh):
    return jax.shard_map(
        on_device,
        mesh=mesh,
        in_specs=(
            P("ctx", "tp"),
            P("ctx", "tp"),
            P(None, "tp"),
            P(None, "tp"),
            P(None, "tp"),
            P("ctx", "tp"),
            P("ctx", None),
            P("ctx", None),
            P("ctx", None),
            P("ctx", None),
            P("ctx", "tp"),
            P(),
            P(),
        ),
        out_specs=P("ctx", "tp"),
        check_vma=False,
    )
```

profile of v0, /device:TPU:1, one launch (start us, length us, event | category | flops | bytes accessed | tf_op | source)
XLA Modules:
  0.0 376.6 jit_solution(14605620880003129420)
XLA Ops:
  12.9 32.4 %all_gather.7 = bf16[1024,256]{0,1:T(8,128)(2,1)S(1)} all-gather(bf16[128,256]{0,1:T(8,128)(2,1)S(1)} %pad_maximum_fusion.3), channel_id=1, replica_groups=mesh['ctx'=8,'tp'=16] {'ctx'}, dimensions={0}, use_global_device_ids=true | all-gather | bytes 589824 | tf_op jit(solution)/shard_map/all_gather | solution.py:96
  53.2 34.4 %all-gather.2.cloned.1.call-done = bf16[8192,256]{1,0:T(8,128)(2,1)} async-done(((bf16[1024,256]{1,0:T(8,128)(2,1)}), bf16[8192,256]{1,0:T(8,128)(2,1)}) %all-gather.2.cloned.1.call-update) | async-done | bytes 4194320 | tf_op jit(solution)/shard_map/all_gather | solution.py:90
  87.6 7.5 %pad_maximum_fusion = (bf16[9216,128]{1,0:T(8,128)(2,1)}, bf16[9216,128]{1,0:T(8,128)(2,1)}) fusion(bf16[1024,256]{1,0:T(8,128)(2,1)S(1)} %copy.39, bf16[8192,256]{1,0:T(8,128)(2,1)} %all-gather.2.cloned.1.call-done), kind=kLoop, calls=%fused_computation.71 | loop fusion | flops 9437184 | bytes 9437184 | tf_op jit(solution)/shard_map/concatenate | solution.py:107
  95.1 84.7 %while.31 = (s32[]{:T(128)}, f32[512]{0:T(512)S(1)}, f32[512]{0:T(512)S(1)}, f32[512]{0:T(512)S(1)}, s32[9]{0:T(128)}, /*index=5*/s32[]{:T(128)}, bf16[9,1024,12...) while((s32[]{:T(128)}, f32[512]{0:T(512)S(1)}, ...), condition=%wide.region_9.10_spmd.clone, body=%wide.region_5.9_spmd.clone.sunk | while | flops 277882880 | bytes 15533248 | solution.py:134
  106.8 2.9 fusion.133
  116.2 2.9 fusion.133
  125.6 2.9 fusion.133
  135.0 2.9 fusion.133
  153.9 2.9 fusion.133
  163.3 2.9 fusion.133
  172.7 2.9 fusion.133
  183.6 4.5 %fusion.95 = (bf16[8192,128]{1,0:T(8,128)(2,1)}, bf16[8192,128]{1,0:T(8,128)(2,1)}) fusion(bf16[8192,256]{1,0:T(8,128)(2,1)} %all-gather.2.cloned.1.call-done), kind=kLoop, calls=%fused_computation.154 | loop fusion | bytes 8388608 | tf_op jit(solution)/shard_map/slice | solution.py:170
  188.1 72.3 %while.32 = (s32[]{:T(128)}, f32[512,128]{1,0:T(8,128)}, s32[8]{0:T(128)}, s32[]{:T(128)}, bf16[8,1024,128]{2,1,0:T(8,128)(2,1)}, /*index=5*/bf16[512,128]{1,0:T...) while((s32[]{:T(128)}, f32[512,128]{1,0:T(8,128)}, ...), condition=%wide.region_11.12_spmd.clone, body=%wide.region_10.11_spmd.clone.sunk | while | flops 407050752 | bytes 5787299 | solution.py:167
  193.4 3.7 fusion.144
  202.3 3.8 %fusion.144 = f32[512,128]{1,0:T(8,128)} fusion(f32[1024,512]{1,0:T(8,128)} %fusion.142, bf16[512,128]{1,0:T(8,128)(2,1)S(1)} %get-tuple-element.522, f32[512]{0:T(512)} %get-tuple-element.523, f32[512]{0:T(512)} %get-tuple-element.520, s32[512]{0:T(512)S(1)} %fusion.143, s32[1024]{0:T(1024)S(1)} %iota_add_fusion.6, ...), kind=kOutput, calls=%fused_computation.37.clone.1 | convolution fusion | flops 272826368 | bytes 3289089 | tf_op jit(solution)/shard_map/while/body/eval_jaxpr/dot_general | solution.py:152
  211.4 3.8 %fusion.144 = f32[512,128]{1,0:T(8,128)} fusion(f32[1024,512]{1,0:T(8,128)} %fusion.142, bf16[512,128]{1,0:T(8,128)(2,1)S(1)} %get-tuple-element.522, f32[512]{0:T(512)} %get-tuple-element.523, f32[512]{0:T(512)} %get-tuple-element.520, s32[512]{0:T(512)S(1)} %fusion.143, s32[1024]{0:T(1024)S(1)} %iota_add_fusion.6, ...), kind=kOutput, calls=%fused_computation.37.clone.1 | convolution fusion | flops 272826368 | bytes 3289089 | tf_op jit(solution)/shard_map/while/body/eval_jaxpr/dot_general | solution.py:152
  220.5 3.8 fusion.144
  229.5 3.8 fusion.144
  238.6 3.8 %fusion.144 = f32[512,128]{1,0:T(8,128)} fusion(f32[1024,512]{1,0:T(8,128)} %fusion.142, bf16[512,128]{1,0:T(8,128)(2,1)S(1)} %get-tuple-element.522, f32[512]{0:T(512)} %get-tuple-element.523, f32[512]{0:T(512)} %get-tuple-element.520, s32[512]{0:T(512)S(1)} %fusion.143, s32[1024]{0:T(1024)S(1)} %iota_add_fusion.6, ...), kind=kOutput, calls=%fused_computation.37.clone.1 | convolution fusion | flops 272826368 | bytes 3289089 | tf_op jit(solution)/shard_map/while/body/eval_jaxpr/dot_general | solution.py:152
  247.6 3.8 %fusion.144 = f32[512,128]{1,0:T(8,128)} fusion(f32[1024,512]{1,0:T(8,128)} %fusion.142, bf16[512,128]{1,0:T(8,128)(2,1)S(1)} %get-tuple-element.522, f32[512]{0:T(512)} %get-tuple-element.523, f32[512]{0:T(512)} %get-tuple-element.520, s32[512]{0:T(512)S(1)} %fusion.143, s32[1024]{0:T(1024)S(1)} %iota_add_fusion.6, ...), kind=kOutput, calls=%fused_computation.37.clone.1 | convolution fusion | flops 272826368 | bytes 3289089 | tf_op jit(solution)/shard_map/while/body/eval_jaxpr/dot_general | solution.py:152
  256.6 3.8 fusion.144
  265.3 6.3 %fusion.97 = f32[128,8192]{1,0:T(8,128)S(1)} fusion(bf16[128,512]{0,1:T(8,128)(2,1)S(1)} %bitcast.155, bf16[8192,512]{1,0:T(8,128)(2,1)} %param.19), kind=kOutput, calls=%fused_computation.156 | convolution fusion | flops 1073741824 | bytes 12713984 | tf_op jit(solution)/shard_map/dot_general | solution.py:39
  275.8 60.3 %reduce-scatter.5.cloned.1.call-done = f32[512,128]{0,1:T(8,128)} async-done(((f32[8192,128]{0,1:T(8,128)}), f32[512,128]{0,1:T(8,128)}) %reduce-scatter.5.cloned.1.call-update) | async-done | bytes 262160 | tf_op jit(solution)/shard_map/reduce_scatter | solution.py:189
  337.2 31.0 %all-reduce = (f32[128]{0:T(128)S(1)}, f32[128]{0:T(128)S(1)}) all-reduce(f32[128]{0:T(128)S(1)} %get-tuple-element.240, f32[128]{0:T(128)S(1)} %get-tuple-element.239), channel_id=1, replica_groups=mesh['ctx'=8,'tp'=16] {'tp'}, use_global_device_ids=true, to_apply=%region_17.18 | all-reduce | flops 256 | bytes 2048 | tf_op jit(solution)/shard_map/psum | solution.py:199
  (242 shorter events, 134.7 us)
Async XLA Ops:
  6.5 6.2 %copy-start.14 = (f32[128]{0:T(128)S(1)}, f32[128]{0:T(128)}, u32[]{:S(2)}) copy-start(f32[128]{0:T(128)} %param.28) | copy-start | bytes 1540
  6.5 81.1 %all-gather.2.cloned.1.call-start = ((), (), s32[]{:S(2)}) async-start(), calls=%async_computation.2 | async-start | bytes 4718592 | tf_op jit(solution)/shard_map/all_gather | solution.py:90
  8.3 37.2 %copy-start.12 = (bf16[128,512]{1,0:T(8,128)(2,1)S(1)}, bf16[128,512]{1,0:T(8,128)(2,1)}, u32[]{:S(2)}) copy-start(bf16[128,512]{1,0:T(8,128)(2,1)} %param.22) | copy-start | bytes 393220
  10.4 253.5 %reduce-scatter.3.cloned.1.call-start = ((), (), s32[]{:S(2)}) async-start(), calls=%async_computation.3 | async-start | bytes 1179648 | tf_op jit(solution)/shard_map/reduce_scatter | solution.py:178
  12.7 32.5 %copy-start.20 = (f32[128]{0:T(128)}, f32[128]{0:T(128)S(1)}, u32[]{:S(2)}) copy-start(f32[128]{0:T(128)S(1)} %get-tuple-element.304) | copy-start | bytes 1540
  45.3 134.5 %copy-start.2 = (bf16[1024,256]{0,1:T(8,128)(2,1)}, bf16[1024,256]{0,1:T(8,128)(2,1)S(1)}, u32[]{:S(2)}) copy-start(bf16[1024,256]{0,1:T(8,128)(2,1)S(1)} %all_gather.7) | copy-start | bytes 1572868
  95.1 84.7 %copy-start.16 = (s32[1024]{0:T(1024)S(1)}, s32[1024]{0:T(1024)}, u32[]{:S(2)}) copy-start(s32[1024]{0:T(1024)} %iota_add_fusion.2) | copy-start | bytes 12292
  95.1 84.7 %copy-start.19 = (s32[512]{0:T(512)S(1)}, s32[512]{0:T(512)}, u32[]{:S(2)}) copy-start(s32[512]{0:T(512)} %fusion.88) | copy-start | bytes 6148
  95.1 84.7 %copy-start.22 = (pred[1024]{0:T(1024)(128)(4,1)S(1)}, pred[1024]{0:T(1024)(128)(4,1)}, u32[]{:S(2)}) copy-start(pred[1024]{0:T(1024)(128)(4,1)} %broadcast_compare_fusion.2) | copy-start | bytes 3076
  100.3 2.3 copy-start.1
  109.7 2.3 copy-start.1
  128.5 2.3 copy-start.1
  183.6 152.6 %reduce-scatter.5.cloned.1.call-start = ((), (), s32[]{:S(2)}) async-start(), calls=%async_computation.4 | async-start | bytes 4456448 | tf_op jit(solution)/shard_map/reduce_scatter | solution.py:189
  260.4 3.3 copy-start.15
  260.4 3.3 copy-start.17
  263.9 7.7 %collective-permute-start = (f32[128,256]{0,1:T(8,128)}, f32[128,256]{0,1:T(8,128)S(1)}, u32[]{:S(2)}, u32[]{:S(2)}) collective-permute-start(f32[128,256]{0,1:T(8,128)} %reduce-scatter.3.cloned.1.call-done), channel_id=1, source_target_pairs={{0,1},{1,0},{2,3},{3,2},{4,5},{5,4},{6,7},{7,6},{8,9},{9,8},{10,11... | collective-permute-start | bytes 393224 | tf_op jit(solution)/shard_map/ppermute | solution.py:20
  265.3 6.4 %copy-start.11 = (f32[128,256]{0,1:T(8,128)S(1)}, f32[128,256]{0,1:T(8,128)}, u32[]{:S(2)}) copy-start(f32[128,256]{0,1:T(8,128)} %reduce-scatter.3.cloned.1.call-done) | copy-start | bytes 393220
  265.3 6.4 %copy-start.7 = (bf16[128,128]{0,1:T(8,128)(2,1)S(1)}, bf16[128,128]{0,1:T(8,128)(2,1)}, u32[]{:S(2)}) copy-start(bf16[128,128]{0,1:T(8,128)(2,1)} %copy-done.6) | copy-start | bytes 98308
  265.3 6.5 %copy-start.5 = (bf16[8192,64]{0,1:T(8,128)(2,1)S(1)}, bf16[8192,64]{0,1:T(8,128)(2,1)}, u32[]{:S(2)}) copy-start(bf16[8192,64]{0,1:T(8,128)(2,1)} %param.20) | copy-start | bytes 3145732
  265.3 6.5 %copy-start.10 = (f32[128,128]{0,1:T(8,128)S(1)}, f32[128,128]{0,1:T(8,128)}, u32[]{:S(2)}) copy-start(f32[128,128]{0,1:T(8,128)} %convert_element_type.44) | copy-start | bytes 196612
  265.3 6.5 %copy-start.21 = (f32[128]{0:T(128)S(1)}, f32[128]{0:T(128)}, u32[]{:S(2)}) copy-start(f32[128]{0:T(128)} %copy-done.20) | copy-start | bytes 1540
  265.3 6.5 %copy-start.23 = (f32[128]{0:T(128)S(1)}, f32[128]{0:T(128)}, u32[]{:S(2)}) copy-start(f32[128]{0:T(128)} %get-tuple-element.303) | copy-start | bytes 1540
  275.8 60.4 %copy-start.8 = (bf16[128,512]{1,0:T(8,128)(2,1)S(1)}, bf16[128,512]{1,0:T(8,128)(2,1)}, u32[]{:S(2)}) copy-start(bf16[128,512]{1,0:T(8,128)(2,1)} %param.17) | copy-start | bytes 393220
  275.8 60.4 %copy-start.9 = (bf16[128,512]{1,0:T(8,128)(2,1)S(1)}, bf16[128,512]{1,0:T(8,128)(2,1)}, u32[]{:S(2)}) copy-start(bf16[128,512]{1,0:T(8,128)(2,1)} %param.18) | copy-start | bytes 393220
  (12 other events, 21.7 us)
Sparse Core Ops, SparseCore 0:
  10.5 77.0 all-gather.1
  183.7 68.0 reduce-scatter.2
  275.9 60.1 reduce-scatter.4
where the time goes:
time: 379 us; the launch traced here: 377 us
  matrix products  108 us (28%)
  waiting for transfers between devices  94.8 us (25%)
  blocking collectives  63.5 us (17%)
  other arithmetic  62 us (16%)
  local copies, waits for them, and re-layouts  31.5 us (8%)
  between operations  14.2 us (4%)
    dot_general x31, matrix products, contract_last(): lax.dot_general(left, right, (((1,), (1,)), ((), ())), preferred_element_...  75.3 us
    reduce_scatter x1, waiting for transfers between devices, on_device(): lax.psum_scatter(contract_last(w_query, grad_q) + contract_last(w_key, gr...  60.3 us
    all_gather x1, waiting for transfers between devices, on_device(): lax.all_gather(jnp.concatenate([unit_rows(raw_keys, s_qk).astype(jnp.bflo...  34.4 us
    all_gather x1, blocking collectives, on_device(): all_window = lax.all_gather(window_pack, 'ctx', axis=0, tiled=True)  32.4 us
    psum x1, blocking collectives, on_device(): lax.psum((jnp.sum(resid * resid, axis=1), jnp.sum(grad_total * resid, axi...  31 us
    dot_general x8, matrix products, cache_step(): jnp.dot(dscores, key_block, preferred_element_type=jnp.float32)  30.1 us
    reduce_sum x9, other arithmetic, stat_step(): row_sum = row_sum * rescale + jnp.sum(expo, axis=1)  20.7 us
    add x18, other arithmetic, block_scores(): key_pos = start + jnp.arange(block, dtype=jnp.int32)  11.1 us
  transfers between devices with their start and end apart: 4, of which 2 were waited for; matrix products, arithmetic and copies ran while one was open for 25% of the time, Pallas kernels for 0%

commit v1 on v0

--- a/solution.py
+++ b/solution.py
@@ -87,11 +87,9 @@
         jnp.float32
     )
     raw_values = lax.dynamic_slice(cache_v, (0, group_index * HD), (cache_rows, HD))
-    all_cache = lax.all_gather(
-        jnp.concatenate([unit_rows(raw_keys, s_qk).astype(jnp.bfloat16), raw_values], 1),
-        "ctx",
-        axis=0,
-        tiled=True,
+    t0 = jnp.concatenate([unit_rows(raw_keys, s_qk).astype(jnp.bfloat16), raw_values], 1)
+    all_cache = jnp.concatenate(
+        lax.all_to_all(jnp.stack([t0 for _ in range(lax.axis_size("ctx"))], axis=0), "ctx", 0, 0), 0
     )
     all_window = lax.all_gather(window_pack, "ctx", axis=0, tiled=True)
     query_raw = q_raw.astype(jnp.float32).reshape(tok_rows, head_count, HD)

time: 379 us -> 401 us (1.058)
  blocking collectives: 63.5 us -> 100 us
  waiting for transfers between devices: 94.8 us -> 59.7 us
  starting transfers between devices: 1.47 us -> 15 us
  local copies, waits for them, and re-layouts: 31.5 us -> 35.7 us
    all_gather x1, blocking collectives: 32.4 us -> 69 us  [on_device(): all_window = lax.all_gather(window_pack, 'ctx', axis=0, tiled=True)]
    all_gather x1 -> x0, waiting for transfers between devices: 34.4 us -> none  [on_device(): lax.all_gather(jnp.concatenate([unit_rows(raw_keys, s_qk).astype(jnp.bflo...]
    all_to_all x0 -> x1, starting transfers between devices: none -> 8.45 us  [on_device(): lax.all_to_all(jnp.stack([t0 for _ in range(lax.axis_size('ctx'))], axis=...]
    ppermute x1, starting transfers between devices: 1.39 us -> 6.44 us  [swapped(): return lax.ppermute(block, axis, route)]
  transfers between devices with their start and end apart: 4 -> 4, of which waited for: 2 -> 1; matrix products, arithmetic and copies ran while one was open for 25% -> 23% of each run, Pallas kernels for 0% -> 0%
where the time goes in v1:
time: 401 us; the launch traced here: 399 us
  matrix products  108 us (27%)
  blocking collectives  100 us (25%)
  other arithmetic  65 us (16%)
  waiting for transfers between devices  59.7 us (15%)
  local copies, waits for them, and re-layouts  35.7 us (9%)
  starting transfers between devices  15 us (4%)
  between operations  14.5 us (4%)
    dot_general x31, matrix products, contract_last(): lax.dot_general(left, right, (((1,), (1,)), ((), ())), preferred_element_...  75.1 us
    all_gather x1, blocking collectives, on_device(): all_window = lax.all_gather(window_pack, 'ctx', axis=0, tiled=True)  69 us
    reduce_scatter x1, waiting for transfers between devices, on_device(): lax.psum_scatter(contract_last(w_query, grad_q) + contract_last(w_key, gr...  59.6 us
    psum x1, blocking collectives, on_device(): lax.psum((jnp.sum(resid * resid, axis=1), jnp.sum(grad_total * resid, axi...  31 us
    dot_general x8, matrix products, cache_step(): jnp.dot(dscores, key_block, preferred_element_type=jnp.float32)  30.1 us
    reduce_sum x9, other arithmetic, stat_step(): row_sum = row_sum * rescale + jnp.sum(expo, axis=1)  20.7 us
    ge x18, other arithmetic, block_scores(): key_pos[None, :] >= floor_pos  12.9 us
    add x18, other arithmetic, block_scores(): key_pos = start + jnp.arange(block, dtype=jnp.int32)  12.9 us
  transfers between devices with their start and end apart: 4, of which 1 were waited for; matrix products, arithmetic and copies ran while one was open for 23% of the time, Pallas kernels for 0%

profile of v1, /device:TPU:1, one launch (start us, length us, event | category | flops | bytes accessed | tf_op | source)
XLA Modules:
  0.0 398.7 jit_solution(2435167038408281762)
XLA Ops:
  11.8 8.5 %all-to-all-start = ((bf16[8,1024,256]{2,1,0:T(8,128)(2,1)}), bf16[8,1024,256]{2,1,0:T(8,128)(2,1)}, u32[]{:S(2)}, u32[]{:S(2)}) async-start(bf16[8,1024,256]{2,1,0:T(8,128)(2,1)} %stack.2), calls=%async_computation | async-start | bytes 8388608 | tf_op jit(solution)/shard_map/all_to_all | solution.py:92
  22.8 69.0 %all_gather.3 = bf16[1024,256]{0,1:T(8,128)(2,1)S(1)} all-gather(bf16[128,256]{0,1:T(8,128)(2,1)S(1)} %pad_maximum_fusion.3), channel_id=1, replica_groups=mesh['ctx'=8,'tp'=16] {'ctx'}, dimensions={0}, use_global_device_ids=true | all-gather | bytes 589824 | tf_op jit(solution)/shard_map/all_gather | solution.py:94
  100.1 4.5 %fusion.95 = (bf16[8192,128]{1,0:T(8,128)(2,1)}, bf16[8192,128]{1,0:T(8,128)(2,1)}) fusion(bf16[8192,256]{1,0:T(8,128)(2,1)} %bitcast.2), kind=kLoop, calls=%fused_computation.154 | loop fusion | bytes 8388608 | tf_op jit(solution)/shard_map/slice | solution.py:168
  104.6 7.5 %pad_maximum_fusion = (bf16[9216,128]{1,0:T(8,128)(2,1)}, bf16[9216,128]{1,0:T(8,128)(2,1)}) fusion(bf16[1024,256]{1,0:T(8,128)(2,1)S(1)} %copy.39, bf16[8192,256]{1,0:T(8,128)(2,1)} %bitcast.2), kind=kLoop, calls=%fused_computation.71 | loop fusion | flops 9437184 | bytes 9437184 | tf_op jit(solution)/shard_map/concatenate | solution.py:105
  112.1 88.1 %while.31 = (s32[]{:T(128)}, f32[512]{0:T(512)S(1)}, f32[512]{0:T(512)S(1)}, f32[512]{0:T(512)S(1)}, s32[9]{0:T(128)}, /*index=5*/s32[]{:T(128)}, bf16[9,1024,12...) while((s32[]{:T(128)}, f32[512]{0:T(512)S(1)}, ...), condition=%wide.region_9.10_spmd.clone, body=%wide.region_5.9_spmd.clone.sunk | while | flops 277882880 | bytes 15533248 | solution.py:132
  144.2 2.9 fusion.133
  154.0 2.9 fusion.133
  163.8 2.9 fusion.133
  173.6 2.9 fusion.133
  183.4 2.9 fusion.133
  193.2 2.9 fusion.133
  204.1 73.9 %while.32 = (s32[]{:T(128)}, f32[512,128]{1,0:T(8,128)}, s32[8]{0:T(128)}, s32[]{:T(128)}, bf16[8,1024,128]{2,1,0:T(8,128)(2,1)}, /*index=5*/bf16[512,128]{1,0:T...) while((s32[]{:T(128)}, f32[512,128]{1,0:T(8,128)}, ...), condition=%wide.region_11.12_spmd.clone, body=%wide.region_10.11_spmd.clone.sunk | while | flops 407050752 | bytes 5787299 | solution.py:165
  209.6 3.7 fusion.144
  218.7 3.8 fusion.144
  227.9 3.8 fusion.144
  237.2 3.8 fusion.144
  246.4 3.8 fusion.144
  255.7 3.8 fusion.144
  264.9 3.8 fusion.144
  274.2 3.8 fusion.144
  281.4 6.4 %collective-permute-start = (f32[128,256]{0,1:T(8,128)}, f32[128,256]{0,1:T(8,128)S(1)}, u32[]{:S(2)}, u32[]{:S(2)}) collective-permute-start(f32[128,256]{0,1:T(8,128)} %reduce-scatter.3.cloned.1.call-done), channel_id=1, source_target_pairs={{0,1},{1,0},{2,3},{3,2},{4,5},{5,4},{6,7},{7,6},{8,9},{9,8},{10,11... | collective-permute-start | bytes 393224 | tf_op jit(solution)/shard_map/ppermute | solution.py:20
  287.9 6.3 %fusion.97 = f32[128,8192]{1,0:T(8,128)S(1)} fusion(bf16[128,512]{0,1:T(8,128)(2,1)S(1)} %bitcast.156, bf16[8192,512]{1,0:T(8,128)(2,1)} %param.19), kind=kOutput, calls=%fused_computation.156 | convolution fusion | flops 1073741824 | bytes 12713984 | tf_op jit(solution)/shard_map/dot_general | solution.py:39
  298.4 59.6 %reduce-scatter.5.cloned.1.call-done = f32[512,128]{0,1:T(8,128)} async-done(((f32[8192,128]{0,1:T(8,128)}), f32[512,128]{0,1:T(8,128)}) %reduce-scatter.5.cloned.1.call-update) | async-done | bytes 262160 | tf_op jit(solution)/shard_map/reduce_scatter | solution.py:187
  359.1 31.0 %all-reduce = (f32[128]{0:T(128)S(1)}, f32[128]{0:T(128)S(1)}) all-reduce(f32[128]{0:T(128)S(1)} %get-tuple-element.240, f32[128]{0:T(128)S(1)} %get-tuple-element.239), channel_id=1, replica_groups=mesh['ctx'=8,'tp'=16] {'tp'}, use_global_device_ids=true, to_apply=%region_17.18 | all-reduce | flops 256 | bytes 2048 | tf_op jit(solution)/shard_map/psum | solution.py:197
  (242 shorter events, 143.3 us)
Async XLA Ops:
  11.8 10.9 %copy-start.14 = (f32[128]{0:T(128)S(1)}, f32[128]{0:T(128)}, u32[]{:S(2)}) copy-start(f32[128]{0:T(128)} %param.28) | copy-start | bytes 1540
  11.8 88.3 %all-to-all-start = ((bf16[8,1024,256]{2,1,0:T(8,128)(2,1)}), bf16[8,1024,256]{2,1,0:T(8,128)(2,1)}, u32[]{:S(2)}, u32[]{:S(2)}) async-start(bf16[8,1024,256]{2,1,0:T(8,128)(2,1)} %stack.2), calls=%async_computation | async-start | bytes 8388608 | tf_op jit(solution)/shard_map/all_to_all | solution.py:92
  20.2 71.7 %copy-start.12 = (bf16[128,512]{1,0:T(8,128)(2,1)S(1)}, bf16[128,512]{1,0:T(8,128)(2,1)}, u32[]{:S(2)}) copy-start(bf16[128,512]{1,0:T(8,128)(2,1)} %param.22) | copy-start | bytes 393220
  20.2 261.2 %reduce-scatter.3.cloned.1.call-start = ((), (), s32[]{:S(2)}) async-start(), calls=%async_computation.3 | async-start | bytes 1179648 | tf_op jit(solution)/shard_map/reduce_scatter | solution.py:176
  22.7 69.1 %copy-start.20 = (f32[128]{0:T(128)}, f32[128]{0:T(128)S(1)}, u32[]{:S(2)}) copy-start(f32[128]{0:T(128)S(1)} %get-tuple-element.304) | copy-start | bytes 1540
  91.8 108.5 %copy-start.2 = (bf16[1024,256]{0,1:T(8,128)(2,1)}, bf16[1024,256]{0,1:T(8,128)(2,1)S(1)}, u32[]{:S(2)}) copy-start(bf16[1024,256]{0,1:T(8,128)(2,1)S(1)} %all_gather.3) | copy-start | bytes 1572868
  112.1 88.2 %copy-start.16 = (s32[1024]{0:T(1024)S(1)}, s32[1024]{0:T(1024)}, u32[]{:S(2)}) copy-start(s32[1024]{0:T(1024)} %iota_add_fusion.2) | copy-start | bytes 12292
  112.1 88.2 %copy-start.19 = (s32[512]{0:T(512)S(1)}, s32[512]{0:T(512)}, u32[]{:S(2)}) copy-start(s32[512]{0:T(512)} %fusion.88) | copy-start | bytes 6148
  112.1 88.2 %copy-start.22 = (pred[1024]{0:T(1024)(128)(4,1)S(1)}, pred[1024]{0:T(1024)(128)(4,1)}, u32[]{:S(2)}) copy-start(pred[1024]{0:T(1024)(128)(4,1)} %broadcast_compare_fusion.2) | copy-start | bytes 3076
  117.7 2.3 copy-start.1
  127.5 2.3 copy-start.1
  147.1 2.3 copy-start.1
  204.0 154.0 %reduce-scatter.5.cloned.1.call-start = ((), (), s32[]{:S(2)}) async-start(), calls=%async_computation.4 | async-start | bytes 4456448 | tf_op jit(solution)/shard_map/reduce_scatter | solution.py:187
  277.9 3.3 copy-start.15
  277.9 3.3 copy-start.17
  281.4 12.8 %collective-permute-start = (f32[128,256]{0,1:T(8,128)}, f32[128,256]{0,1:T(8,128)S(1)}, u32[]{:S(2)}, u32[]{:S(2)}) collective-permute-start(f32[128,256]{0,1:T(8,128)} %reduce-scatter.3.cloned.1.call-done), channel_id=1, source_target_pairs={{0,1},{1,0},{2,3},{3,2},{4,5},{5,4},{6,7},{7,6},{8,9},{9,8},{10,11... | collective-permute-start | bytes 393224 | tf_op jit(solution)/shard_map/ppermute | solution.py:20
  287.9 6.4 %copy-start.11 = (f32[128,256]{0,1:T(8,128)S(1)}, f32[128,256]{0,1:T(8,128)}, u32[]{:S(2)}) copy-start(f32[128,256]{0,1:T(8,128)} %reduce-scatter.3.cloned.1.call-done) | copy-start | bytes 393220
  287.9 6.4 %copy-start.7 = (bf16[128,128]{0,1:T(8,128)(2,1)S(1)}, bf16[128,128]{0,1:T(8,128)(2,1)}, u32[]{:S(2)}) copy-start(bf16[128,128]{0,1:T(8,128)(2,1)} %copy-done.6) | copy-start | bytes 98308
  287.9 6.5 %copy-start.5 = (bf16[8192,64]{0,1:T(8,128)(2,1)S(1)}, bf16[8192,64]{0,1:T(8,128)(2,1)}, u32[]{:S(2)}) copy-start(bf16[8192,64]{0,1:T(8,128)(2,1)} %param.20) | copy-start | bytes 3145732
  287.9 6.5 %copy-start.10 = (f32[128,128]{0,1:T(8,128)S(1)}, f32[128,128]{0,1:T(8,128)}, u32[]{:S(2)}) copy-start(f32[128,128]{0,1:T(8,128)} %convert_element_type.44) | copy-start | bytes 196612
  287.9 6.5 %copy-start.21 = (f32[128]{0:T(128)S(1)}, f32[128]{0:T(128)}, u32[]{:S(2)}) copy-start(f32[128]{0:T(128)} %copy-done.20) | copy-start | bytes 1540
  287.9 6.5 %copy-start.23 = (f32[128]{0:T(128)S(1)}, f32[128]{0:T(128)}, u32[]{:S(2)}) copy-start(f32[128]{0:T(128)} %get-tuple-element.303) | copy-start | bytes 1540
  298.3 59.6 %copy-start.8 = (bf16[128,512]{1,0:T(8,128)(2,1)S(1)}, bf16[128,512]{1,0:T(8,128)(2,1)}, u32[]{:S(2)}) copy-start(bf16[128,512]{1,0:T(8,128)(2,1)} %param.17) | copy-start | bytes 393220
  298.3 59.6 %copy-start.9 = (bf16[128,512]{1,0:T(8,128)(2,1)S(1)}, bf16[128,512]{1,0:T(8,128)(2,1)}, u32[]{:S(2)}) copy-start(bf16[128,512]{1,0:T(8,128)(2,1)} %param.18) | copy-start | bytes 393220
  (12 other events, 21.7 us)
Sparse Core Ops, SparseCore 0:
  204.1 72.4 reduce-scatter.2
  298.5 59.4 reduce-scatter.4
